TPU v7x, 512 devices: a whole 4x4x16 slice. The times are simulated.
512 devices in a mesh: lat: 32 (over z, core), lev: 16 (over x, y).
Axes of the slice: x: 4, y: 4, z: 16, core: 2. Of those that a mesh axis runs over, the one named last changes fastest.
Arguments:
- zonal_wind: float32 [64, 256, 2880], P('lev', 'lat'), may hold values from -1 to 1
- merid_wind: float32 [64, 256, 2880], P('lev', 'lat'), may hold values from -1 to 1
- thickness: float32 [64, 256, 2880], P('lev', 'lat'), may hold values from 0.6 to 1.8
- potential_temp: float32 [64, 256, 2880], P('lev', 'lat'), may hold values from 0.5 to 2
- cutoff: int32 [32], replicated, may hold values from 4 to 255, as said below
- sigma_weights: float32 [64], replicated, may hold values from 0.5 to 2
Outputs:
- remapped_wind: float32 [64, 256, 2880], P(None, 'lat', 'lev')
- remapped_temp: float32 [64, 256, 2880], P(None, 'lat', 'lev')
Inputs may be any that keep to these rules, and one draw needn't show every extreme that they name: `cutoff`: cutoff wavenumber of each filtered row, southern rows in row order, then northern rows in row order.
All inputs are finite; a program needn't handle non-finite values.
Results may differ from a plain program's by a relative error of at most 0.0003.
Values sent between devices are 32-bit elements; how exact they have to be, the bound alone decides.
No kernel may reach another device: no remote copies, remote signals or barrier semaphores. Data moves between devices by JAX's collectives and lax.ppermute only.
A program may use at most 64 MiB of HBM per device.

v0:
```python
import math
import jax
import jax.numpy as jnp
from jax import lax
from jax.sharding import PartitionSpec as P

POLAR_BANDS = 2
KMAX = 256
COURANT = 0.02
PRESSURE_COEF = 0.05
HIGHEST = lax.Precision.HIGHEST


def with_halo(x, sides, width):
    for axis, dim in sides:
        count, length = (lax.axis_size(axis), x.shape[dim])
        up = [(i, (i + 1) % count) for i in range(count - 1)]
        down = [(j, i) for i, j in up]
        last = lax.slice_in_dim(x, length - width, length, axis=dim)
        first = lax.slice_in_dim(x, 0, width, axis=dim)
        before = lax.ppermute(last, axis, up)
        after = lax.ppermute(first, axis, down)
        x = jnp.concatenate([before, x, after], axis=dim)
    return x


def prefix(part, axis, combine, identity):
    place = lax.axis_index(axis)
    gathered = lax.all_gather(part, axis)
    state = jnp.zeros_like(part) + jnp.asarray(identity, part.dtype)

    def one(lap, state):
        return combine(state, lax.dynamic_index_in_dim(gathered, lap, 0, False))

    return lax.fori_loop(0, place, one, state)


def flux_zonal(quantity, wind):
    face_wind = 0.5 * (wind + jnp.roll(wind, 1, axis=-1))
    face_flux = face_wind * 0.5 * (quantity + jnp.roll(quantity, 1, axis=-1))
    return jnp.roll(face_flux, -1, axis=-1) - face_flux


def flux_merid(padded_field, padded_wind):
    face_flux = (
        0.25
        * (padded_wind[:, :-1] + padded_wind[:, 1:])
        * (padded_field[:, :-1] + padded_field[:, 1:])
    )
    return face_flux[:, 1:] - face_flux[:, :-1]


def advance(thickness, potential, zonal, merid_pad, thick_pad, temp_pad):
    heat = thickness * potential
    heat_pad = thick_pad * temp_pad
    new_thick = thickness - COURANT * (
        flux_zonal(thickness, zonal) + flux_merid(thick_pad, merid_pad)
    )
    new_heat = heat - COURANT * (flux_zonal(heat, zonal) + flux_merid(heat_pad, merid_pad))
    return (new_thick, new_heat / new_thick)


def pressure_push(zonal, mid_pressure):
    return zonal - PRESSURE_COEF * (
        jnp.roll(mid_pressure, -1, axis=-1) - jnp.roll(mid_pressure, 1, axis=-1)
    )


def ppm_edges(fields):
    halves = 0.5 * (fields[:, :-1] + fields[:, 1:])
    fourth = 7.0 / 12.0 * (fields[:, 1:-2] + fields[:, 2:-1]) - 1.0 / 12.0 * (
        fields[:, :-3] + fields[:, 3:]
    )
    return jnp.concatenate(
        [fields[:, :1], halves[:, :1], fourth, halves[:, -1:], fields[:, -1:]], axis=1
    )


def remap_columns(fields, thickness, weights):
    levels = thickness.shape[0]
    field_count = fields.shape[0]
    flat_thick = thickness.reshape(levels, -1)
    flat_fields = fields.reshape(field_count, levels, -1)
    top_edges = jnp.cumsum(flat_thick, axis=0) - flat_thick
    surface = jnp.sum(flat_thick, axis=0)
    sigma_edges = (jnp.cumsum(weights) / jnp.sum(weights))[:, None]
    targets = surface[None] * sigma_edges
    previous = jnp.concatenate([jnp.zeros_like(targets[:1]), targets[:-1]], axis=0)
    edge_values = ppm_edges(flat_fields)
    left_edge = edge_values[:, :-1]
    curvature = 6.0 * (flat_fields - 0.5 * (left_edge + edge_values[:, 1:]))
    linear = edge_values[:, 1:] - left_edge + curvature

    def mass_block(edge_block):
        fraction = jnp.clip((edge_block[:, None] - top_edges[None]) / flat_thick[None], 0.0, 1.0)
        collected = []
        for member in range(field_count):
            partial_value = fraction * (
                left_edge[member][None]
                + fraction * (0.5 * linear[member][None] - fraction * curvature[member][None] / 3.0)
            )
            collected.append(jnp.sum(flat_thick[None] * partial_value, axis=1))
        return tuple(collected)

    grouped = targets.reshape(levels // 8, 8, -1)
    masses = lax.map(mass_block, grouped)
    results = []
    for mass in masses:
        mass_below = mass.reshape(levels, -1)
        mass_above = jnp.concatenate([jnp.zeros_like(mass_below[:1]), mass_below[:-1]], axis=0)
        results.append((mass_below - mass_above) / (targets - previous))
    return jnp.stack(results).reshape(fields.shape)


def modes_table(first_wave, wave_count, lon_count):
    wavenumber = first_wave + lax.iota(jnp.int32, wave_count)
    position = lax.iota(jnp.int32, lon_count)
    phase_index = wavenumber[:, None] * position[None, :] % lon_count
    angles = phase_index.astype(jnp.float32) * (2.0 * math.pi / lon_count)
    return (jnp.concatenate([jnp.cos(angles), jnp.sin(angles)], axis=0), wavenumber)


def weighted_spectrum(vectors, limits, modes, wavenumber):
    lon_count = vectors.shape[-1]
    spectrum = jnp.einsum("vi,ki->vk", vectors, modes, precision=HIGHEST)
    factor = jnp.where(wavenumber == 0, 1.0, 2.0) / lon_count
    kept_weight = jnp.where(wavenumber[None, :] <= limits[:, None], factor[None, :], 0.0)
    kept_weight = jnp.concatenate([kept_weight, kept_weight], axis=1)
    return spectrum * kept_weight


def filter_part(vectors, limits, first_wave, wave_count):
    modes, wavenumber = modes_table(first_wave, wave_count, vectors.shape[-1])
    weighted = weighted_spectrum(vectors, limits, modes, wavenumber)
    return jnp.dot(weighted, modes, precision=HIGHEST, preferred_element_type=jnp.float32)


def add_terms(earlier, later):
    return earlier + later


def local(zonal_wind, merid_wind, thickness, potential_temp, cutoff, sigma_weights):
    levels_dev, rows_dev, lon_count = zonal_wind.shape
    band_count = lax.axis_size("lat")
    band_index = lax.axis_index("lat")
    polar_rows = POLAR_BANDS * rows_dev
    all_rows = band_count * rows_dev
    wind_pair = jnp.stack([zonal_wind, merid_wind])
    southern = band_index < POLAR_BANDS
    is_polar = jnp.logical_or(southern, band_index >= band_count - POLAR_BANDS)
    offset = jnp.where(
        southern, band_index * rows_dev, band_index * rows_dev - all_rows + 2 * polar_rows
    )
    offset = jnp.clip(offset, 0, 2 * polar_rows - rows_dev)
    own_limits = lax.dynamic_slice_in_dim(cutoff, offset, rows_dev)
    limits = jnp.broadcast_to(own_limits, (2, levels_dev, rows_dev)).reshape(-1)

    def smoothed(wind_block):
        flat_rows = wind_block.reshape(-1, lon_count)
        return filter_part(flat_rows, limits, 0, KMAX).reshape(wind_block.shape)

    def unchanged(wind_block):
        return wind_block

    wind_pair = lax.cond(is_polar, smoothed, unchanged, wind_pair)
    zonal = wind_pair[0]
    stacked = jnp.stack([thickness, wind_pair[1], potential_temp])
    padded = with_halo(stacked, (("lat", 2),), 1)
    new_thick, new_temp = advance(thickness, potential_temp, zonal, padded[1], padded[0], padded[2])
    own_mass = jnp.sum(new_thick, axis=0)
    upper_mass = prefix(own_mass, "lev", add_terms, jnp.zeros_like(own_mass))
    mid_pressure = upper_mass[None] + jnp.cumsum(new_thick, axis=0) - 0.5 * new_thick
    new_zonal = pressure_push(zonal, mid_pressure)
    outgoing = jnp.stack([new_zonal, new_temp, new_thick])
    columns = lax.all_to_all(outgoing, "lev", split_axis=3, concat_axis=1, tiled=True)
    result = remap_columns(columns[:2], columns[2], sigma_weights)
    return (result[0], result[1])


def solution(mesh):
    in_specs = (
        P("lev", "lat", None),
        P("lev", "lat", None),
        P("lev", "lat", None),
        P("lev", "lat", None),
        P(),
        P(),
    )
    out_specs = (P(None, "lat", "lev"), P(None, "lat", "lev"))
    return jax.shard_map(local, mesh=mesh, in_specs=in_specs, out_specs=out_specs, check_vma=False)
```

profile of v0, /device:TPU:32, one launch (start us, length us, event | category | flops | bytes accessed | tf_op | source)
XLA Modules:
  0.0 282.6 jit_solution(11586409146098346025)
XLA Ops:
  7.2 2.0 pad_maximum_fusion.11
  9.3 1.2 slice_bitcast_fusion.9
  10.5 1.3 pad_maximum_fusion.14
  11.8 1.9 collective-permute-start
  13.8 27.1 %collective-permute-start.1 = (f32[3,4,1,2880]{3,1,2,0:T(4,128)S(1)}, f32[3,4,1,2880]{3,1,2,0:T(4,128)S(1)}, u32[]{:S(2)}, u32[]{:S(2)}) collective-permute-start(f32[3,4,1,2880]{3,1,2,0:T(4,128)S(1)} %copy.84), channel_id=1, source_target_pairs={{16,0},{32,16},{48,32},{64,48},{80,64},{96,80},{112,96},{128,112},... | collective-permute-start | bytes 414728 | tf_op jit(solution)/shard_map/ppermute | solution.py:22
  41.2 1.4 fusion.36
  44.4 0.8 fusion.37
  45.4 62.9 %all-gather.3.cloned.1.call-done = f32[128,2880]{1,0:T(8,128)} async-done(((f32[8,2880]{1,0:T(8,128)}), f32[128,2880]{1,0:T(8,128)}) %all-gather.3.cloned.1.call-update) | async-done | bytes 1474576 | tf_op jit(solution)/shard_map/all_gather | solution.py:29
  108.4 2.4 fusion.15
  111.0 1.2 fusion.35
  112.3 12.1 %copy.79 = f32[3,4,8,2880]{2,1,0,3:T(4,128)} copy(f32[3,4,8,2880]{3,2,1,0:T(8,128)S(1)} %pad_maximum_fusion.8) | data formatting | bytes 2211840 | tf_op jit(solution)/shard_map/stack | solution.py:174
  124.4 22.8 %reshape.137 = f32[16,1,17280]{2,1,0:T(1,128)} reshape(f32[2880,3,4,8]{3,2,1,0:T(4,128)} %bitcast.101) | data formatting | bytes 2211840
  147.2 18.2 %all-to-all-start = ((f32[16,1,17280]{2,1,0:T(1,128)}), f32[16,1,17280]{2,1,0:T(1,128)S(1)}, u32[]{:S(2)}, u32[]{:S(2)}) async-start(f32[16,1,17280]{2,1,0:T(1,128)} %reshape.137), calls=%async_computation | async-start | bytes 2211840 | tf_op jit(solution)/shard_map/all_to_all | solution.py:175
  166.2 0.8 divide_reduce_fusion
  167.0 14.3 %all-to-all-done = f32[16,1,17280]{2,1,0:T(1,128)S(1)} async-done(((f32[16,1,17280]{2,1,0:T(1,128)}), f32[16,1,17280]{2,1,0:T(1,128)S(1)}, u32[]{:S(2)}, u32[]{:S(2)}) %all-to-all-start) | async-done | bytes 1105952 | tf_op jit(solution)/shard_map/all_to_all | solution.py:175
  181.9 3.3 %reduce.4 = f32[16,17280]{1,0:T(8,128)S(1)} reduce(f32[16,1,17280]{2,1,0:T(1,128)S(1)} %all-to-all-done, f32[]{:T(128)} %broadcast.115), dimensions={1}, to_apply=%all_to_all.11.reduce_sub_computation | reduce | bytes 2211844 | tf_op jit(solution)/shard_map/all_to_all | solution.py:175
  185.2 27.2 %reshape.138 = f32[2880,3,4,8]{3,2,1,0:T(4,128)} reshape(f32[16,17280]{1,0:T(8,128)S(1)} %reduce.4) | data formatting | bytes 2211840
  212.4 12.9 %copy.80 = f32[3,4,8,16,180]{4,2,1,3,0:T(8,128)S(1)} copy(f32[3,4,8,16,180]{2,1,0,4,3:T(4,128)} %bitcast.100) | data formatting | bytes 2211840 | tf_op jit(solution)/shard_map/all_to_all | solution.py:175
  225.3 1.1 slice.252
  226.3 1.6 reshape.131
  228.4 0.9 slice_reduce_fusion
  229.7 1.3 reshape_squeeze.3
  231.0 1.1 reduce_window_sum.30
  232.1 1.0 sub.102
  233.2 0.9 broadcast_multiply_fusion
  234.1 0.8 broadcast_multiply_fusion.1
  234.9 1.3 mul.381
  236.2 35.5 %while.24 = (s32[]{:T(128)}, f32[8,8,1440]{2,1,0:T(8,128)}, f32[8,8,1440]{2,1,0:T(8,128)}, f32[1,64,8,180]{3,2,1,0:T(8,128)}, f32[8,8,1440]{2,1,0:T(8,128)}, /*i...) while((s32[]{:T(128)}, f32[8,8,1440]{2,1,0:T(8,128)}, ...), condition=%wide.wide.region_13.14_spmd, body=%wide.wide.region_10.13_spmd.sunk | while | flops 14169602 | bytes 7794801 | solution.py:106
  236.3 0.8 dynamic-slice_bitcast_fusion.3
  237.2 2.2 multiply_reduce_fusion.4
  239.4 0.6 bitcast_dynamic-update-slice_fusion.7
  240.8 0.8 dynamic-slice_bitcast_fusion.3
  241.6 2.2 multiply_reduce_fusion.4
  245.2 0.8 dynamic-slice_bitcast_fusion.3
  246.1 2.2 multiply_reduce_fusion.4
  249.6 0.8 dynamic-slice_bitcast_fusion.3
  250.5 2.2 multiply_reduce_fusion.4
  254.1 0.8 dynamic-slice_bitcast_fusion.3
  255.0 2.2 multiply_reduce_fusion.4
  258.5 0.8 dynamic-slice_bitcast_fusion.3
  259.4 2.2 multiply_reduce_fusion.4
  263.0 0.8 dynamic-slice_bitcast_fusion.3
  263.8 2.2 multiply_reduce_fusion.4
  267.4 0.8 dynamic-slice_bitcast_fusion.3
  268.3 2.2 multiply_reduce_fusion.4
  271.7 1.7 subtract_divide_fusion
  273.4 1.2 squeeze.28
  274.6 1.2 squeeze.29
  (77 shorter events, 15.9 us)
Async XLA Ops:
  7.2 101.2 %all-gather.3.cloned.1.call-start = ((), (), s32[]{:S(2)}) async-start(), calls=%async_computation.1 | async-start | bytes 1601536 | tf_op jit(solution)/shard_map/all_gather | solution.py:29
  9.3 1.2 copy-start.1
  9.3 31.6 %copy-start.2 = (f32[4,8,2880]{2,1,0:T(8,128)S(1)}, f32[4,8,2880]{2,1,0:T(8,128)}, u32[]{:S(2)}) copy-start(f32[4,8,2880]{2,1,0:T(8,128)} %param.15) | copy-start | bytes 1105924
  11.8 30.8 %collective-permute-start = (f32[3,4,1,2880]{3,1,2,0:T(4,128)S(1)}, f32[3,4,1,2880]{3,1,2,0:T(4,128)S(1)}, u32[]{:S(2)}, u32[]{:S(2)}) collective-permute-start(f32[3,4,1,2880]{3,1,2,0:T(4,128)S(1)} %copy.83), channel_id=1, source_target_pairs={{0,16},{16,32},{32,48},{48,64},{64,80},{80,96},{96,112},{112,128},... | collective-permute-start | bytes 414728 | tf_op jit(solution)/shard_map/ppermute | solution.py:21
  13.8 29.5 %collective-permute-start.1 = (f32[3,4,1,2880]{3,1,2,0:T(4,128)S(1)}, f32[3,4,1,2880]{3,1,2,0:T(4,128)S(1)}, u32[]{:S(2)}, u32[]{:S(2)}) collective-permute-start(f32[3,4,1,2880]{3,1,2,0:T(4,128)S(1)} %copy.84), channel_id=1, source_target_pairs={{16,0},{32,16},{48,32},{64,48},{80,64},{96,80},{112,96},{128,112},... | collective-permute-start | bytes 414728 | tf_op jit(solution)/shard_map/ppermute | solution.py:22
  124.4 41.0 %copy-start.3 = (f32[64]{0:T(128)S(1)}, f32[64]{0:T(128)}, u32[]{:S(2)}) copy-start(f32[64]{0:T(128)} %param.17) | copy-start | bytes 772
  147.2 34.2 %all-to-all-start = ((f32[16,1,17280]{2,1,0:T(1,128)}), f32[16,1,17280]{2,1,0:T(1,128)S(1)}, u32[]{:S(2)}, u32[]{:S(2)}) async-start(f32[16,1,17280]{2,1,0:T(1,128)} %reshape.137), calls=%async_computation | async-start | bytes 2211840 | tf_op jit(solution)/shard_map/all_to_all | solution.py:175
Sparse Core Ops, SparseCore 0:
  45.3 63.0 all-gather.2
where the time goes:
time: 284 us; the launch traced here: 283 us
  local copies, waits for them, and re-layouts  103 us (36%)
  waiting for transfers between devices  77.7 us (27%)
  starting transfers between devices  47.2 us (17%)
  other arithmetic  40.5 us (14%)
  between operations  14.3 us (5%)
    all_gather x1, waiting for transfers between devices, prefix(): gathered = lax.all_gather(part, axis)  62.9 us
    unnamed x10, local copies, waits for them, and re-layouts  50.1 us
    ppermute x1, starting transfers between devices, with_halo(): after = lax.ppermute(first, axis, down)  27.1 us
    all_to_all x1, starting transfers between devices, local(): lax.all_to_all(outgoing, 'lev', split_axis=3, concat_axis=1, tiled=True)  18.2 us
    reduce_sum x8, other arithmetic, mass_block(): collected.append(jnp.sum(flat_thick[None] * partial_value, axis=1))  17.5 us
    all_to_all x1, waiting for transfers between devices, local(): lax.all_to_all(outgoing, 'lev', split_axis=3, concat_axis=1, tiled=True)  14.3 us
    all_to_all x2, local copies, waits for them, and re-layouts, local(): lax.all_to_all(outgoing, 'lev', split_axis=3, concat_axis=1, tiled=True)  13.4 us
    another operation x1, local copies, waits for them, and re-layouts, local(): outgoing = jnp.stack([new_zonal, new_temp, new_thick])  12.1 us
  transfers between devices with their start and end apart: 4, of which 3 were waited for; matrix products, arithmetic and copies ran while one was open for 1% of the time, Pallas kernels for 0%

commit v1 on v0

--- a/solution.py
+++ b/solution.py
@@ -140,6 +140,15 @@
 
 
 def local(zonal_wind, merid_wind, thickness, potential_temp, cutoff, sigma_weights):
+
+    def connect_thing(in_array):
+        return jnp.concatenate(
+            jax.lax.all_to_all(
+                jnp.stack(jnp.split(in_array, jax.lax.axis_size("lev"), 3)), "lev", 0, 0
+            ),
+            axis=1,
+        )
+
     levels_dev, rows_dev, lon_count = zonal_wind.shape
     band_count = lax.axis_size("lat")
     band_index = lax.axis_index("lat")
@@ -172,7 +181,7 @@
     mid_pressure = upper_mass[None] + jnp.cumsum(new_thick, axis=0) - 0.5 * new_thick
     new_zonal = pressure_push(zonal, mid_pressure)
     outgoing = jnp.stack([new_zonal, new_temp, new_thick])
-    columns = lax.all_to_all(outgoing, "lev", split_axis=3, concat_axis=1, tiled=True)
+    columns = connect_thing(outgoing)
     result = remap_columns(columns[:2], columns[2], sigma_weights)
     return (result[0], result[1])
 

time: 284 us -> 218 us (0.77)
  local copies, waits for them, and re-layouts: 103 us -> 34.2 us
  waiting for transfers between devices: 77.7 us -> 83.1 us
  other arithmetic: 40.5 us -> 37.3 us
    unnamed x10 -> x25, local copies, waits for them, and re-layouts: 50.1 us -> 10.9 us
    all_to_all x2 -> x0, local copies, waits for them, and re-layouts: 13.4 us -> none  [local(): lax.all_to_all(outgoing, 'lev', split_axis=3, concat_axis=1, tiled=True)]
    another operation x1, local copies, waits for them, and re-layouts: 12.1 us -> 0.73 us  [connect_thing(): jnp.stack(jnp.split(in_array, jax.lax.axis_size('lev'), 3))]
    all_to_all x1, waiting for transfers between devices: 14.3 us -> 19.4 us  [connect_thing(): jax.lax.all_to_all(jnp.stack(jnp.split(in_array, jax.lax.axis_size('lev')...]
    dynamic_update_slice x16, local copies, waits for them, and re-layouts: 9.97 us -> 5.08 us  [remap_columns(): masses = lax.map(mass_block, grouped)]
    all_to_all x1 -> x0, other arithmetic: 3.27 us -> none  [local(): lax.all_to_all(outgoing, 'lev', split_axis=3, concat_axis=1, tiled=True)]
  transfers between devices with their start and end apart: 4 -> 4, of which waited for: 3 -> 3; matrix products, arithmetic and copies ran while one was open for 1% -> 2% of each run, Pallas kernels for 0% -> 0%
where the time goes in v1:
time: 218 us; the launch traced here: 216 us
  waiting for transfers between devices  83.1 us (38%)
  starting transfers between devices  47.2 us (22%)
  other arithmetic  37.3 us (17%)
  local copies, waits for them, and re-layouts  34.2 us (16%)
  between operations  14.3 us (7%)
    all_gather x1, waiting for transfers between devices, prefix(): gathered = lax.all_gather(part, axis)  62.9 us
    ppermute x1, starting transfers between devices, with_halo(): after = lax.ppermute(first, axis, down)  26.9 us
    all_to_all x1, waiting for transfers between devices, connect_thing(): jax.lax.all_to_all(jnp.stack(jnp.split(in_array, jax.lax.axis_size('lev')...  19.4 us
    all_to_all x1, starting transfers between devices, connect_thing(): jax.lax.all_to_all(jnp.stack(jnp.split(in_array, jax.lax.axis_size('lev')...  18.3 us
    reduce_sum x8, other arithmetic, mass_block(): collected.append(jnp.sum(flat_thick[None] * partial_value, axis=1))  17.5 us
    unnamed x25, local copies, waits for them, and re-layouts  10.9 us
    sub x8, local copies, waits for them, and re-layouts, mass_block(): edge_block[:, None] - top_edges[None]  6.47 us
    dynamic_update_slice x16, local copies, waits for them, and re-layouts, remap_columns(): masses = lax.map(mass_block, grouped)  5.08 us
  transfers between devices with their start and end apart: 4, of which 3 were waited for; matrix products, arithmetic and copies ran while one was open for 2% of the time, Pallas kernels for 0%

profile of v1, /device:TPU:32, one launch (start us, length us, event | category | flops | bytes accessed | tf_op | source)
XLA Modules:
  0.0 216.3 jit_solution(9129141795702191568)
XLA Ops:
  7.2 2.0 pad_maximum_fusion.11
  9.3 1.2 slice_bitcast_fusion.9
  10.8 1.9 collective-permute-start
  12.7 26.9 %collective-permute-start.1 = (f32[3,4,1,2880]{3,2,1,0:T(1,128)S(1)}, f32[3,4,1,2880]{3,2,1,0:T(1,128)S(1)}, u32[]{:S(2)}, u32[]{:S(2)}) collective-permute-start(f32[3,4,1,2880]{3,2,1,0:T(1,128)S(1)} %get-tuple-element.179), channel_id=1, source_target_pairs={{16,0},{32,16},{48,32},{64,48},{80,64},{96,80},{112,96},{128,112},... | collective-permute-start | bytes 414728 | tf_op jit(solution)/shard_map/ppermute | solution.py:22
  39.9 1.4 fusion.36
  41.4 0.8 collective-permute-done.1
  43.1 0.8 fusion.53
  44.2 62.9 %all-gather.3.cloned.1.call-done = f32[128,2880]{1,0:T(8,128)} async-done(((f32[8,2880]{1,0:T(8,128)}), f32[128,2880]{1,0:T(8,128)}) %all-gather.3.cloned.1.call-update) | async-done | bytes 1474576 | tf_op jit(solution)/shard_map/all_gather | solution.py:29
  107.1 2.4 %fusion.15 = f32[4,8,2880]{2,1,0:T(8,128)S(1)} fusion(f32[4,8,2880]{2,1,0:T(8,128)S(1)} %get-tuple-element.159, f32[8,2880]{1,0:T(8,128)S(1)} %get-tuple-element.125), kind=kOutput, calls=%fused_computation.34 | output fusion | flops 552960 | bytes 829440 | tf_op jit(solution)/shard_map/jit(cumsum)/reduce_window_sum | solution.py:181
  109.8 1.2 fusion.35
  112.4 0.7 fusion.50
  113.1 0.7 fusion.49
  113.9 0.7 fusion.48
  116.8 0.7 fusion.44
  119.0 0.7 fusion.41
  120.4 0.7 fusion.39
  122.6 18.3 %all-to-all-start = ((f32[16,3,4,8,180]{4,3,2,1,0:T(8,128)}), f32[16,3,4,8,180]{4,3,2,1,0:T(8,128)S(1)}, u32[]{:S(2)}, u32[]{:S(2)}) async-start(f32[16,3,4,8,180]{4,3,2,1,0:T(8,128)} %fusion.37), calls=%async_computation | async-start | bytes 3145728 | tf_op jit(solution)/shard_map/all_to_all | solution.py:146
  141.7 0.8 divide_reduce_fusion
  143.2 19.4 %all-to-all-done = f32[16,3,4,8,180]{4,3,2,1,0:T(8,128)S(1)} async-done(((f32[16,3,4,8,180]{4,3,2,1,0:T(8,128)}), f32[16,3,4,8,180]{4,3,2,1,0:T(8,128)S(1)}, u32[]{:S(2)}, u32[]{:S(2)}) %all-to-all-start) | async-done | bytes 1105952 | tf_op jit(solution)/shard_map/all_to_all | solution.py:146
  162.7 1.1 copy.20
  163.7 1.6 reshape.136
  165.8 0.9 slice_reduce_fusion
  167.2 1.3 reshape_squeeze.3
  168.4 1.1 reduce_window_sum.30
  169.5 1.0 sub.102
  170.6 1.5 broadcast_multiply_fusion
  172.1 1.5 broadcast_multiply_fusion.1
  173.7 1.3 mul.381
  174.9 30.7 %while.24 = (s32[]{:T(128)}, f32[8,8,1440]{2,1,0:T(8,128)S(1)}, f32[8,8,1440]{2,1,0:T(8,128)}, f32[1,64,8,180]{3,2,1,0:T(8,128)}, f32[8,8,1440]{2,1,0:T(8,128)},...) while((s32[]{:T(128)}, f32[8,8,1440]{2,1,0:T(8,128)S(1)}, ...), condition=%wide.wide.region_13.14_spmd, body=%wide.wide.region_10.13_spmd.sunk | while | flops 14169602 | bytes 7797365 | solution.py:106
  175.1 0.8 dynamic-slice_bitcast_fusion.3
  175.9 2.2 %multiply_reduce_fusion.4 = (f32[8,1440]{1,0:T(8,128)S(1)}, f32[8,1440]{1,0:T(8,128)S(1)}) fusion(f32[64,1440]{1,0:T(8,128)S(1)} %get-tuple-element.335, f32[64,1440]{1,0:T(8,128)S(1)} %get-tuple-element.336, f32[64,1440]{1,0:T(8,128)S(1)} %get-tuple-element.337, f32[64,1440]{1,0:T(8,128)S(1)} %get-tuple-element.391, ...), kind=kLoop, calls=%fused_computation.21.clone.clone.1 | loop fusion | flops 13985280 | bytes 3087360 | tf_op jit(solution)/shard_map/while/body/eval_jaxpr/reduce_sum | solution.py:102
  178.9 0.8 dynamic-slice_bitcast_fusion.3
  179.8 2.2 %multiply_reduce_fusion.4 = (f32[8,1440]{1,0:T(8,128)S(1)}, f32[8,1440]{1,0:T(8,128)S(1)}) fusion(f32[64,1440]{1,0:T(8,128)S(1)} %get-tuple-element.335, f32[64,1440]{1,0:T(8,128)S(1)} %get-tuple-element.336, f32[64,1440]{1,0:T(8,128)S(1)} %get-tuple-element.337, f32[64,1440]{1,0:T(8,128)S(1)} %get-tuple-element.391, ...), kind=kLoop, calls=%fused_computation.21.clone.clone.1 | loop fusion | flops 13985280 | bytes 3087360 | tf_op jit(solution)/shard_map/while/body/eval_jaxpr/reduce_sum | solution.py:102
  182.7 0.8 dynamic-slice_bitcast_fusion.3
  183.6 2.2 %multiply_reduce_fusion.4 = (f32[8,1440]{1,0:T(8,128)S(1)}, f32[8,1440]{1,0:T(8,128)S(1)}) fusion(f32[64,1440]{1,0:T(8,128)S(1)} %get-tuple-element.335, f32[64,1440]{1,0:T(8,128)S(1)} %get-tuple-element.336, f32[64,1440]{1,0:T(8,128)S(1)} %get-tuple-element.337, f32[64,1440]{1,0:T(8,128)S(1)} %get-tuple-element.391, ...), kind=kLoop, calls=%fused_computation.21.clone.clone.1 | loop fusion | flops 13985280 | bytes 3087360 | tf_op jit(solution)/shard_map/while/body/eval_jaxpr/reduce_sum | solution.py:102
  186.6 0.8 dynamic-slice_bitcast_fusion.3
  187.4 2.2 %multiply_reduce_fusion.4 = (f32[8,1440]{1,0:T(8,128)S(1)}, f32[8,1440]{1,0:T(8,128)S(1)}) fusion(f32[64,1440]{1,0:T(8,128)S(1)} %get-tuple-element.335, f32[64,1440]{1,0:T(8,128)S(1)} %get-tuple-element.336, f32[64,1440]{1,0:T(8,128)S(1)} %get-tuple-element.337, f32[64,1440]{1,0:T(8,128)S(1)} %get-tuple-element.391, ...), kind=kLoop, calls=%fused_computation.21.clone.clone.1 | loop fusion | flops 13985280 | bytes 3087360 | tf_op jit(solution)/shard_map/while/body/eval_jaxpr/reduce_sum | solution.py:102
  190.4 0.8 dynamic-slice_bitcast_fusion.3
  191.3 2.2 %multiply_reduce_fusion.4 = (f32[8,1440]{1,0:T(8,128)S(1)}, f32[8,1440]{1,0:T(8,128)S(1)}) fusion(f32[64,1440]{1,0:T(8,128)S(1)} %get-tuple-element.335, f32[64,1440]{1,0:T(8,128)S(1)} %get-tuple-element.336, f32[64,1440]{1,0:T(8,128)S(1)} %get-tuple-element.337, f32[64,1440]{1,0:T(8,128)S(1)} %get-tuple-element.391, ...), kind=kLoop, calls=%fused_computation.21.clone.clone.1 | loop fusion | flops 13985280 | bytes 3087360 | tf_op jit(solution)/shard_map/while/body/eval_jaxpr/reduce_sum | solution.py:102
  194.3 0.8 dynamic-slice_bitcast_fusion.3
  195.1 2.2 %multiply_reduce_fusion.4 = (f32[8,1440]{1,0:T(8,128)S(1)}, f32[8,1440]{1,0:T(8,128)S(1)}) fusion(f32[64,1440]{1,0:T(8,128)S(1)} %get-tuple-element.335, f32[64,1440]{1,0:T(8,128)S(1)} %get-tuple-element.336, f32[64,1440]{1,0:T(8,128)S(1)} %get-tuple-element.337, f32[64,1440]{1,0:T(8,128)S(1)} %get-tuple-element.391, ...), kind=kLoop, calls=%fused_computation.21.clone.clone.1 | loop fusion | flops 13985280 | bytes 3087360 | tf_op jit(solution)/shard_map/while/body/eval_jaxpr/reduce_sum | solution.py:102
  198.1 0.8 dynamic-slice_bitcast_fusion.3
  199.0 2.2 %multiply_reduce_fusion.4 = (f32[8,1440]{1,0:T(8,128)S(1)}, f32[8,1440]{1,0:T(8,128)S(1)}) fusion(f32[64,1440]{1,0:T(8,128)S(1)} %get-tuple-element.335, f32[64,1440]{1,0:T(8,128)S(1)} %get-tuple-element.336, f32[64,1440]{1,0:T(8,128)S(1)} %get-tuple-element.337, f32[64,1440]{1,0:T(8,128)S(1)} %get-tuple-element.391, ...), kind=kLoop, calls=%fused_computation.21.clone.clone.1 | loop fusion | flops 13985280 | bytes 3087360 | tf_op jit(solution)/shard_map/while/body/eval_jaxpr/reduce_sum | solution.py:102
  201.9 0.8 dynamic-slice_bitcast_fusion.3
  202.8 2.2 %multiply_reduce_fusion.4 = (f32[8,1440]{1,0:T(8,128)S(1)}, f32[8,1440]{1,0:T(8,128)S(1)}) fusion(f32[64,1440]{1,0:T(8,128)S(1)} %get-tuple-element.335, f32[64,1440]{1,0:T(8,128)S(1)} %get-tuple-element.336, f32[64,1440]{1,0:T(8,128)S(1)} %get-tuple-element.337, f32[64,1440]{1,0:T(8,128)S(1)} %get-tuple-element.391, ...), kind=kLoop, calls=%fused_computation.21.clone.clone.1 | loop fusion | flops 13985280 | bytes 3087360 | tf_op jit(solution)/shard_map/while/body/eval_jaxpr/reduce_sum | solution.py:102
  205.6 1.5 subtract_divide_fusion
  207.1 1.2 squeeze.28
  208.3 1.2 squeeze.29
  (88 shorter events, 18.4 us)
Async XLA Ops:
  7.2 99.9 %all-gather.3.cloned.1.call-start = ((), (), s32[]{:S(2)}) async-start(), calls=%async_computation.1 | async-start | bytes 1601536 | tf_op jit(solution)/shard_map/all_gather | solution.py:29
  9.3 1.2 copy-start.1
  9.3 1.3 copy-start.2
  10.8 30.6 %collective-permute-start = (f32[3,4,1,2880]{3,2,1,0:T(1,128)S(1)}, f32[3,4,1,2880]{3,2,1,0:T(1,128)S(1)}, u32[]{:S(2)}, u32[]{:S(2)}) collective-permute-start(f32[3,4,1,2880]{3,2,1,0:T(1,128)S(1)} %get-tuple-element.178), channel_id=1, source_target_pairs={{0,16},{16,32},{32,48},{48,64},{64,80},{80,96},{96,112},{112,128},... | collective-permute-start | bytes 414728 | tf_op jit(solution)/shard_map/ppermute | solution.py:21
  12.7 29.5 %collective-permute-start.1 = (f32[3,4,1,2880]{3,2,1,0:T(1,128)S(1)}, f32[3,4,1,2880]{3,2,1,0:T(1,128)S(1)}, u32[]{:S(2)}, u32[]{:S(2)}) collective-permute-start(f32[3,4,1,2880]{3,2,1,0:T(1,128)S(1)} %get-tuple-element.179), channel_id=1, source_target_pairs={{16,0},{32,16},{48,32},{64,48},{80,64},{96,80},{112,96},{128,112},... | collective-permute-start | bytes 414728 | tf_op jit(solution)/shard_map/ppermute | solution.py:22
  122.6 18.4 %copy-start.5 = (f32[64]{0:T(128)S(1)}, f32[64]{0:T(128)}, u32[]{:S(2)}) copy-start(f32[64]{0:T(128)} %param.17) | copy-start | bytes 772
  122.6 40.0 %all-to-all-start = ((f32[16,3,4,8,180]{4,3,2,1,0:T(8,128)}), f32[16,3,4,8,180]{4,3,2,1,0:T(8,128)S(1)}, u32[]{:S(2)}, u32[]{:S(2)}) async-start(f32[16,3,4,8,180]{4,3,2,1,0:T(8,128)} %fusion.37), calls=%async_computation | async-start | bytes 3145728 | tf_op jit(solution)/shard_map/all_to_all | solution.py:146
  142.5 21.2 %copy-start.3 = (f32[64]{0:T(128)}, f32[64]{0:T(128)S(1)}, u32[]{:S(2)}) copy-start(f32[64]{0:T(128)S(1)} %divide_reduce_fusion) | copy-start | bytes 772
  174.9 30.7 %copy-start.4 = (f32[64]{0:T(128)S(1)}, f32[64]{0:T(128)}, u32[]{:S(2)}) copy-start(f32[64]{0:T(128)} %copy-done.3) | copy-start | bytes 772
Sparse Core Ops, SparseCore 0:
  44.0 63.0 all-gather.2
